TPU v7x, 32 devices: a whole 2x2x4 slice. The times are simulated.
32 devices in a mesh: row: 4 (over y, x), col: 8 (over z, core).
Axes of the slice: x: 2, y: 2, z: 4, core: 2. Of those that a mesh axis runs over, the one named last changes fastest.
Arguments:
- inverses: bfloat16 [4, 32, 1024, 1024], P('row', 'col'), as said below
- coupling: bfloat16 [4, 32, 1024, 256], P('row', 'col'), may hold values from -0.1875 to 0.1875
- orders: int32 [4, 32], P('row', 'col'), may hold values from 512 to 1024, as said below
- owners: int32 [4, 32, 1], P(None, 'col'), may hold values from 0 to 3, as said below
- offsets: int32 [4, 32, 2], P(None, 'col'), may hold values from 0 to 2
- dense_slab: float32 [2048, 4096], P('row', 'col'), may hold values from -6 to 6
- pivots: float32 [1024], replicated, may hold values from 16 to 128
Outputs:
- result: float32 [2048, 4096], P('row', 'col')
Inputs may be any that keep to these rules, and one draw needn't show every extreme that they name: `orders`: order of each subdomain; some subdomain has exactly 1024. `owners`: within the 4 subdomains of one device (entries r, s with the same r and the same s // 4) no row block is named twice. `inverses`: each inverse is symmetric.
All inputs are finite; a program needn't handle non-finite values.
Results may differ from a plain program's by a relative error of at most 0.0035.
Values may be sent and summed in bfloat16 or wider, within the bound.
A program may use at most 64 MiB of HBM per device.

v0:
```python
import functools
import jax
import jax.numpy as jnp
from jax import lax
from jax.experimental import pallas as pl
from jax.experimental.pallas import tpu as pltpu
from jax.sharding import PartitionSpec as P

MESH = pl.DeviceIdType.MESH
BF16 = jnp.bfloat16
F32 = jnp.float32
CHUNKS = 16
MERGE = 2
AB = 256


def contract0(a, b):
    return lax.dot_general(a, b, (((0,), (0,)), ((), ())), preferred_element_type=F32)


def kernel(
    dims,
    inv_hbm, cpl_hbm, orders, owners, offsets, slab_hbm, pivots,
    out,
    a_buf, m_buf, slab, mm, sol, send, recv, placed, panel, left, piv,
    a_sem, m_sem, s_sem, t_send, t_recv, ax_send, ay_send, g_recv,
    up_send, dn_send, core_send, l_recv,
):
    rows, cols, subs, order, width, tile = dims
    unit = (tile - width) // 2
    nb = width // unit
    grid = tile // unit
    pairs = [(a, b) for a in range(nb) for b in range(a, nb)]
    chunk = tile // CHUNKS
    ablocks = order // AB

    r = lax.axis_index("row")
    c = lax.axis_index("col")
    q, core = lax.div(c, 2), lax.rem(c, 2)
    chips = cols // 2
    q0, k0 = lax.div(r, 2), lax.rem(r, 2)
    pa = lax.rem(r, 2)
    pb = 1 - pa
    mate = r + 1 - 2 * pa
    on_line = core == k0
    diag = (q == q0) & on_line
    has_up = on_line & (q >= q0) & (q + 1 < chips)
    has_dn = on_line & (q <= q0) & (q > 0)
    chip_hops = jnp.where(q >= q0, q - q0, q0 - q)

    def load_a(s, i):
        return pltpu.make_async_copy(
            inv_hbm.at[0, s, pl.ds(i * AB, AB), pl.ds(i * AB, order - i * AB)],
            a_buf.at[s, pl.ds(i * AB, AB), pl.ds(i * AB, order - i * AB)],
            a_sem.at[s, i])

    def load_m(s):
        return pltpu.make_async_copy(cpl_hbm.at[0, s], m_buf.at[s], m_sem.at[s])

    load_slab = pltpu.make_async_copy(slab_hbm, slab, s_sem)
    for s in range(subs):
        load_m(s).start()
        for i in range(ablocks):
            load_a(s, i).start()
    load_slab.start()

    barrier = pltpu.get_barrier_semaphore()
    for t in range(rows):
        @pl.when(t != r)
        def _():
            pl.semaphore_signal(barrier, inc=1, device_id=(t, c), device_id_type=MESH)
    pl.semaphore_signal(barrier, inc=1, device_id=(r, c + 1 - 2 * core), device_id_type=MESH)

    @pl.when(q + 1 < chips)
    def _():
        pl.semaphore_signal(barrier, inc=1, device_id=(r, c + 2), device_id_type=MESH)

    @pl.when(q > 0)
    def _():
        pl.semaphore_signal(barrier, inc=1, device_id=(r, c - 2), device_id_type=MESH)

    for k in range(pivots.shape[0]):
        piv[pl.ds(k * 128, 128), :] = jnp.transpose(
            jnp.broadcast_to(pivots[pl.ds(k, 1), :], (128, 128)))
    for t in range(rows):
        for k in range(nb + 1):
            placed[t, k * (nb + 1) + nb] = jnp.zeros((unit, unit), BF16)
            placed[t, nb * (nb + 1) + k] = jnp.zeros((unit, unit), BF16)

    neighbours = rows + jnp.where(q + 1 < chips, 1, 0) + jnp.where(q > 0, 1, 0)
    pl.semaphore_wait(barrier, neighbours)

    def pick(src, dst):
        found, which = jnp.int32(0), jnp.int32(0)
        for s in range(subs):
            hit = owners[src, 0, s] == dst
            found, which = jnp.where(hit, 1, found), jnp.where(hit, s, which)
        return found, which

    def tile_copy(t, src_row):
        return pltpu.make_async_remote_copy(
            src_ref=send.at[t], dst_ref=recv.at[src_row],
            send_sem=t_send.at[t], recv_sem=t_recv.at[src_row],
            device_id=(t, c), device_id_type=MESH)

    for s in range(subs):
        load_m(s).wait()
        for i in range(ablocks):
            load_a(s, i).wait()

    for t in range(rows):
        _, which = pick(r, t)
        live = lax.broadcasted_iota(jnp.int32, (order, width), 0) < orders[0, which]
        mm[...] = jnp.where(live, m_buf[which], jnp.zeros((order, width), BF16))
        for i in range(ablocks):
            lo = i * AB
            half = a_buf[which, lo:lo + AB, lo:lo + AB] * jnp.asarray(0.5, BF16)
            part = jnp.dot(half, mm[lo:lo + AB], preferred_element_type=F32)
            if i + 1 < ablocks:
                part = part + jnp.dot(a_buf[which, lo:lo + AB, lo + AB:], mm[lo + AB:],
                                      preferred_element_type=F32)
            sol[lo:lo + AB] = part.astype(BF16)
        half_tile = contract0(mm[...], sol[...])
        whole_tile = (half_tile + jnp.transpose(half_tile)).astype(BF16)
        value = jnp.stack([whole_tile[a * unit:(a + 1) * unit, b * unit:(b + 1) * unit]
                           for a, b in pairs])

        @pl.when(t != r)
        def _():
            send[t] = value
            tile_copy(t, r).start()

        @pl.when(t == r)
        def _():
            recv[t] = value

    def part(ref, p, j):
        return ref.at[p, pl.ds(pl.multiple_of(j * chunk, chunk), chunk)]

    def panel_copy(j, target, sems):
        return pltpu.make_async_remote_copy(
            src_ref=part(panel, pa, j), dst_ref=part(panel, pa, j),
            send_sem=sems.at[j], recv_sem=g_recv.at[pa, j],
            device_id=(target, c), device_id_type=MESH)

    def panel_got(p, j):
        pltpu.make_async_remote_copy(
            src_ref=part(panel, p, j), dst_ref=part(panel, p, j),
            send_sem=ax_send.at[j], recv_sem=g_recv.at[p, j],
            device_id=(mate, c), device_id_type=MESH).wait_recv()

    def send_panel(j):
        @pl.when(r + 2 < rows)
        def _():
            panel_copy(j, r + 2, ay_send).start()
        panel_copy(j, mate, ax_send).start()

    def left_copy(src, p, j, target, sems):
        return pltpu.make_async_remote_copy(
            src_ref=part(src, p, j), dst_ref=part(left, p, j),
            send_sem=sems.at[p, j], recv_sem=l_recv.at[p, j],
            device_id=(r, target), device_id_type=MESH)

    def forward(src, p, j):
        @pl.when(has_up)
        def _():
            left_copy(src, p, j, c + 2, up_send).start()

        @pl.when(has_dn)
        def _():
            left_copy(src, p, j, c - 2, dn_send).start()
        left_copy(src, p, j, c + 1 - 2 * core, core_send).start()

    load_slab.wait()
    places = []
    side = nb + 1
    for t in range(rows):
        found, which = pick(t, r)
        at_row, at_col = offsets[t, 0, which], offsets[t, 1, which]
        spots = []
        for start in (at_row, at_col):
            inside = [(found > 0) & (k - start >= 0) & (k - start < nb) for k in range(grid)]
            spots.append([jnp.where(ok, k - start, nb) for k, ok in enumerate(inside)])
        places.append(([side * a for a in spots[0]], spots[1]))

        @pl.when(t != r)
        def _():
            tile_copy(t, t).wait_recv()
    for t in range(rows):
        for k, (a, b) in enumerate(pairs):
            value = recv[t, k]
            placed[t, a * side + b] = value
            if a != b:
                placed[t, b * side + a] = jnp.transpose(value.astype(F32)).astype(BF16)
    for i in range(grid):
        for j in range(grid):
            total = slab[i * unit:(i + 1) * unit, j * unit:(j + 1) * unit]
            for t in range(rows):
                total = total - placed[t, places[t][0][i] + places[t][1][j]].astype(F32)
            out[i * unit:(i + 1) * unit, j * unit:(j + 1) * unit] = total

        @pl.when(r < 2)
        def _():
            span = slice(i * unit, (i + 1) * unit)
            panel[pa, span] = out[span, :].astype(BF16)
            for j in range(i * unit // chunk, (i + 1) * unit // chunk):
                send_panel(j)

    lanes = tile // 128
    late = 4
    off_line = jnp.where(on_line, 0, 2)
    first_left = jnp.where(diag | (r < 2), 0, 4 * chip_hops + off_line)

    def step(n, carry):
        @pl.when((n < CHUNKS) & (r >= 2))
        def _():
            panel_got(pa, n)
            send_panel(n)

        def own(p, j):
            @pl.when(diag)
            def _():
                forward(panel, p, j)
                at = pl.ds(pl.multiple_of(j * chunk, chunk), chunk)
                left[p, at] = panel[p, at]

        def other(p, j):
            @pl.when((j >= 0) & (j < CHUNKS) & jnp.logical_not(diag))
            def _():
                left_copy(left, p, j, c + 1 - 2 * core, core_send).wait_recv()

                @pl.when(on_line)
                def _():
                    forward(left, p, j)

        @pl.when(n < CHUNKS)
        def _():
            own(pa, n)
        m = n - late

        @pl.when((m >= 0) & (m < CHUNKS) & diag)
        def _():
            panel_got(pb, m)
            own(pb, m)
        other(pa, n - first_left)
        j = m - first_left
        other(pb, j)

        @pl.when((j >= 0) & jnp.logical_not(diag))
        def _():
            panel_got(pb, j)

        @pl.when((j >= 0) & (lax.rem(j, MERGE) == MERGE - 1))
        def _():
            first = pl.multiple_of((j - (MERGE - 1)) * chunk, MERGE * chunk)
            at = pl.ds(first, MERGE * chunk)
            factors, rights = [], []
            for p in range(2):
                pivot = piv[pl.ds(pl.multiple_of(p * tile + first, chunk), MERGE * chunk), :]
                raw = left[p, at].astype(F32)
                factors.append((raw / jnp.concatenate([pivot] * lanes, axis=1)).astype(BF16))
                rights.append(panel[p, at])
            factor = jnp.concatenate(factors, axis=0)
            out[...] = out[...] - contract0(factor, jnp.concatenate(rights, axis=0))
        return carry

    lax.fori_loop(0, CHUNKS + first_left + late, step, 0)

    for t in range(rows):
        @pl.when(t != r)
        def _():
            tile_copy(t, r).wait_send()

    def drain(j, carry):
        @pl.when(r + 2 < rows)
        def _():
            panel_copy(j, r + 2, ay_send).wait_send()
        panel_copy(j, mate, ax_send).wait_send()

        @pl.when(on_line)
        def _():
            for p in range(2):
                @pl.when(has_up)
                def _():
                    left_copy(left, p, j, c + 2, up_send).wait_send()

                @pl.when(has_dn)
                def _():
                    left_copy(left, p, j, c - 2, dn_send).wait_send()
                left_copy(left, p, j, c + 1 - 2 * core, core_send).wait_send()
        return carry

    lax.fori_loop(0, CHUNKS, drain, 0)


def body(rows, cols, inverses, coupling, orders, owners, offsets, dense_slab, pivots):
    subs, order = inverses.shape[1], inverses.shape[2]
    width, tile = coupling.shape[3], dense_slab.shape[0]
    unit = (tile - width) // 2
    nb = width // unit
    upper = nb * (nb + 1) // 2
    panel_width = pivots.shape[0]
    assert panel_width == 2 * tile and rows % 2 == 0 and cols % 2 == 0
    dma = pltpu.SemaphoreType.DMA
    hbm = pl.BlockSpec(memory_space=pl.ANY)
    smem = pl.BlockSpec(memory_space=pltpu.SMEM)
    vmem = pl.BlockSpec(memory_space=pltpu.VMEM)
    return pl.pallas_call(
        functools.partial(kernel, (rows, cols, subs, order, width, tile)),
        out_shape=pltpu.VMEM((tile, tile), F32),
        in_specs=[hbm, hbm, smem, smem, smem, hbm, vmem],
        out_specs=vmem,
        scratch_shapes=[
            pltpu.VMEM((subs, order, order), BF16),
            pltpu.VMEM((subs, order, width), BF16),
            pltpu.VMEM((tile, tile), F32),
            pltpu.VMEM((order, width), BF16),
            pltpu.VMEM((order, width), BF16),
            pltpu.VMEM((rows, upper, unit, unit), BF16),
            pltpu.VMEM((rows, upper, unit, unit), BF16),
            pltpu.VMEM((rows, (nb + 1) * (nb + 1), unit, unit), BF16),
            pltpu.VMEM((2, tile, tile), BF16),
            pltpu.VMEM((2, tile, tile), BF16),
            pltpu.VMEM((panel_width, 128), F32),
            dma((subs, order // AB)), dma((subs,)), dma(()),
            dma((rows,)), dma((rows,)),
            dma((CHUNKS,)), dma((CHUNKS,)), dma((2, CHUNKS)),
            dma((2, CHUNKS)), dma((2, CHUNKS)), dma((2, CHUNKS)), dma((2, CHUNKS)),
        ],
        compiler_params=pltpu.CompilerParams(collective_id=0, has_side_effects=True),
    )(inverses, coupling, orders, jnp.transpose(owners, (0, 2, 1)),
      jnp.transpose(offsets, (0, 2, 1)), dense_slab, pivots.reshape(-1, 128))


def solution(mesh):
    placed = (
        P("row", "col", None, None),
        P("row", "col", None, None),
        P("row", "col"),
        P(None, "col", None),
        P(None, "col", None),
        P("row", "col"),
        P(),
    )
    return jax.shard_map(
        functools.partial(body, mesh.shape["row"], mesh.shape["col"]),
        mesh=mesh, in_specs=placed, out_specs=P("row", "col"), check_vma=False)
```

profile of v0, /device:TPU:29, one launch (start us, length us, event | category | flops | bytes accessed | tf_op | source)
XLA Modules:
  0.0 38.1 jit_solution(628232208084186272)
XLA Ops:
  0.0 37.1 %shard_map.73 = f32[512,512]{1,0:T(8,128)S(1)} custom-call(bf16[1,4,1024,1024]{3,2,1,0:T(8,128)(2,1)} %inv_hbm.1, bf16[1,4,1024,256]{3,2,1,0:T(8,128)(2,1)} %cpl_hbm.1, s32[1,4]{1,0:T(1,128)} %orders.1, s32[4,1,4]{2,1,0:T(1,128)} %bitcast.7, s32[4,2,4]{2,1,0:T(2,128)} %bitcast.5, f32[512,512]{1,0:T(8,128)} %slab_hbm.1, f32[8,128]{1,0:T(8,128)} %bitcast.6), custom_call_target="tpu_custom_call" | custom-call | tf_op jit(solution)/shard_map/pallas_call | solution.py:308
  37.1 1.0 %copy.10 = f32[512,512]{1,0:T(8,128)} copy(f32[512,512]{1,0:T(8,128)S(1)} %shard_map.73) | data formatting | bytes 2097152
where the time goes:
time: 38.3 us; the launch traced here: 38.1 us
  Pallas kernels  37.1 us (97%)
  local copies, waits for them, and re-layouts  0.97 us (3%)
    pallas_call x1, Pallas kernels, body(): pl.pallas_call(functools.partial(kernel, (rows, cols, subs, order, width,...  37.1 us
    unnamed x1, local copies, waits for them, and re-layouts  0.97 us

commit v1 on v0

v1 whole, which is shorter than its diff:
```python
import functools
import jax
import jax.numpy as jnp
from jax import lax
from jax.experimental import pallas as pl
from jax.experimental.pallas import tpu as pltpu
from jax.sharding import PartitionSpec as P

MESH = pl.DeviceIdType.MESH
BF16 = jnp.bfloat16
F32 = jnp.float32
CHUNKS = 16
MERGE = 2
AB = 256
PAD = 16
HOP_ROW = 8
HOP_COL = 8
HOP_CORE = 5


def contract0(a, b):
    return lax.dot_general(a, b, (((0,), (0,)), ((), ())), preferred_element_type=F32)


def kernel(
    dims,
    inv_hbm, cpl_hbm, orders, owners, offsets, slab_hbm, pivots,
    out,
    a_buf, m_buf, slab, send, recv, placed, panel, left, piv,
    a_sem, m_sem, s_sem, t_send, t_recv, ax_send, ay_send, g_recv,
    up_send, dn_send, core_send, l_recv,
):
    rows, cols, subs, order, width, tile = dims
    unit = (tile - width) // 2
    nb = width // unit
    grid = tile // unit
    pairs = [(a, b) for a in range(nb) for b in range(a + 1, nb)]
    chunk = tile // CHUNKS
    ablocks = order // AB

    r = lax.axis_index("row")
    c = lax.axis_index("col")
    q, core = lax.div(c, 2), lax.rem(c, 2)
    chips = cols // 2
    q0, k0 = lax.div(r, 2), lax.rem(r, 2)
    pa = lax.rem(r, 2)
    pb = 1 - pa
    mate = r + 1 - 2 * pa
    sibling = c + 1 - 2 * core
    on_line = core == k0
    at_source = q == q0
    diag = at_source & on_line
    has_up = (q >= q0) & (q + 1 < chips)
    has_dn = (q <= q0) & (q > 0)
    chip_hops = jnp.where(q >= q0, q - q0, q0 - q)
    pc = jnp.where(on_line, pb, pa)
    po = 1 - pc

    def load_a(s, i):
        return pltpu.make_async_copy(
            inv_hbm.at[0, s, pl.ds(i * AB, AB), pl.ds(i * AB, order - i * AB)],
            a_buf.at[s, pl.ds(i * AB, AB), pl.ds(i * AB, order - i * AB)],
            a_sem.at[s])

    def wait_a(s):
        total = sum(AB * (order - i * AB) for i in range(ablocks)) // order
        pltpu.make_async_copy(
            inv_hbm.at[0, s, pl.ds(0, total)], a_buf.at[s, pl.ds(0, total)], a_sem.at[s]).wait()

    def load_m(s):
        return pltpu.make_async_copy(cpl_hbm.at[0, s], m_buf.at[s], m_sem.at[s])

    load_slab = pltpu.make_async_copy(slab_hbm, slab, s_sem)
    for s in range(subs):
        load_m(s).start()
        for i in range(ablocks):
            load_a(s, i).start()

    barrier = pltpu.get_barrier_semaphore()
    for t in range(rows):
        @pl.when(t != r)
        def _():
            pl.semaphore_signal(barrier, inc=1, device_id=(t, c), device_id_type=MESH)
    pl.semaphore_signal(barrier, inc=1, device_id=(r, sibling), device_id_type=MESH)

    @pl.when(q + 1 < chips)
    def _():
        pl.semaphore_signal(barrier, inc=1, device_id=(r, c + 2), device_id_type=MESH)

    @pl.when(q > 0)
    def _():
        pl.semaphore_signal(barrier, inc=1, device_id=(r, c - 2), device_id_type=MESH)

    def pick(src, dst):
        found, which = jnp.int32(0), jnp.int32(0)
        for s in range(subs):
            hit = owners[src, 0, s] == dst
            found, which = jnp.where(hit, 1, found), jnp.where(hit, s, which)
        return found, which

    def tile_copy(t, src_row):
        return pltpu.make_async_remote_copy(
            src_ref=send.at[t], dst_ref=recv.at[src_row],
            send_sem=t_send, recv_sem=t_recv.at[src_row],
            device_id=(t, c), device_id_type=MESH)

    above = (lax.broadcasted_iota(jnp.int32, (unit, unit), 0)
             <= lax.broadcasted_iota(jnp.int32, (unit, unit), 1))
    equal = (lax.broadcasted_iota(jnp.int32, (unit, unit), 0)
             == lax.broadcasted_iota(jnp.int32, (unit, unit), 1))

    def make_tile(which):
        live = lax.broadcasted_iota(jnp.int32, (order, width), 0) < orders[0, which]
        masked = jnp.where(live, m_buf[which], jnp.zeros((order, width), BF16))
        pieces = []
        for i in range(ablocks):
            lo, hi = i * AB, (i + 1) * AB
            half = a_buf[which, lo:hi, lo:hi] * jnp.asarray(0.5, BF16)
            piece = jnp.dot(half, masked[lo:hi], preferred_element_type=F32)
            if hi < order:
                piece = piece + jnp.dot(a_buf[which, lo:hi, hi:], masked[hi:],
                                        preferred_element_type=F32)
            pieces.append(piece.astype(BF16))
        half_tile = contract0(masked, jnp.concatenate(pieces, axis=0))

        def block(a, b):
            return half_tile[a * unit:(a + 1) * unit, b * unit:(b + 1) * unit]

        def whole(a, b):
            return block(a, b) + jnp.transpose(block(b, a))

        stored = [jnp.where(above, whole(a, a), whole(a + 1, a + 1)) for a in range(0, nb, 2)]
        stored += [whole(a, b) for a, b in pairs]
        stored += [jnp.broadcast_to(jnp.sum(jnp.where(equal, 2 * block(a, a), 0.0), axis=0, keepdims=True),
                                    (PAD, unit)) for a in range(1, nb, 2)]
        return jnp.concatenate(stored, axis=0).astype(BF16)

    for s in range(subs):
        load_m(s).wait()
        wait_a(s)
    load_slab.start()

    neighbours = rows + jnp.where(q + 1 < chips, 1, 0) + jnp.where(q > 0, 1, 0)
    pl.semaphore_wait(barrier, neighbours)

    others = rows - 2
    for u in range(rows):
        if u == 0:
            t = pb
        elif u == rows - 1:
            t = r
        else:
            far = jnp.where(r < 2, 2 + lax.rem(u - 1 + pa, others), 2 + lax.rem(r - 2 + u - 1, others))
            t = jnp.where(r >= 2, pa, far) if u == 1 else far
        _, which = pick(r, t)
        value = make_tile(which)
        if u < rows - 1:
            send[t] = value
            tile_copy(t, r).start()
        else:
            recv[t] = value

    for k in range(pivots.shape[0]):
        piv[pl.ds(k * 128, 128), :] = jnp.transpose(
            jnp.broadcast_to(pivots[pl.ds(k, 1), :], (128, 128)))
    for t in range(rows):
        for k in range(nb + 1):
            placed[t, k * (nb + 1) + nb] = jnp.zeros((unit, unit), BF16)
            placed[t, nb * (nb + 1) + k] = jnp.zeros((unit, unit), BF16)


    def part(ref, p, j):
        return ref.at[p, pl.ds(pl.multiple_of(j * chunk, chunk), chunk)]

    def panel_copy(j, target, sem):
        return pltpu.make_async_remote_copy(
            src_ref=part(panel, pa, j), dst_ref=part(panel, pa, j),
            send_sem=sem, recv_sem=g_recv.at[pa, j],
            device_id=(target, c), device_id_type=MESH)

    def panel_got(p, j):
        pltpu.make_async_remote_copy(
            src_ref=part(panel, p, j), dst_ref=part(panel, p, j),
            send_sem=ax_send, recv_sem=g_recv.at[p, j],
            device_id=(mate, c), device_id_type=MESH).wait_recv()

    def send_panel(j):
        panel_copy(j, mate, ax_send).start()

        @pl.when(r + 2 < rows)
        def _():
            panel_copy(j, r + 2, ay_send).start()

    def left_copy(p, j, target, sem):
        return pltpu.make_async_remote_copy(
            src_ref=part(left, p, j), dst_ref=part(left, p, j),
            send_sem=sem, recv_sem=l_recv.at[p, j],
            device_id=(r, target), device_id_type=MESH)

    def along(j):
        @pl.when(has_up)
        def _():
            left_copy(pc, j, c + 2, up_send).start()

        @pl.when(has_dn)
        def _():
            left_copy(pc, j, c - 2, dn_send).start()

    lanes = tile // 128

    def divide(p, j):
        at = pl.ds(pl.multiple_of(j * chunk, chunk), chunk)
        pivot = piv[pl.ds(pl.multiple_of(p * tile + j * chunk, chunk), chunk), :]
        raw = panel[p, at].astype(F32)
        left[p, at] = (raw / jnp.concatenate([pivot] * lanes, axis=1)).astype(BF16)

    load_slab.wait()
    places = []
    side = nb + 1
    for t in range(rows):
        found, which = pick(t, r)
        at_row, at_col = offsets[t, 0, which], offsets[t, 1, which]
        spots = []
        for start in (at_row, at_col):
            inside = [(found > 0) & (k - start >= 0) & (k - start < nb) for k in range(grid)]
            spots.append([jnp.where(ok, k - start, nb) for k, ok in enumerate(inside)])
        places.append(([side * a for a in spots[0]], spots[1]))

        @pl.when(t != r)
        def _():
            tile_copy(t, t).wait_recv()
    for t in range(rows):
        for k in range(nb // 2):
            pack = recv[t, k * unit:(k + 1) * unit].astype(F32)
            flip = jnp.transpose(pack)
            at = (nb // 2 + len(pairs)) * unit + k * PAD
            line = jnp.concatenate([recv[t, at:at + PAD]] * (unit // PAD), axis=0).astype(F32)
            a = 2 * k
            placed[t, a * side + a] = jnp.where(above, pack, flip).astype(BF16)
            low = jnp.where(above, flip, pack)
            placed[t, (a + 1) * side + a + 1] = jnp.where(equal, line, low).astype(BF16)
        for k, (a, b) in enumerate(pairs):
            at = (nb // 2 + k) * unit
            value = recv[t, at:at + unit]
            placed[t, a * side + b] = value
            placed[t, b * side + a] = jnp.transpose(value.astype(F32)).astype(BF16)
    for i in range(grid):
        for j in range(grid):
            total = slab[i * unit:(i + 1) * unit, j * unit:(j + 1) * unit]
            for t in range(rows):
                total = total - placed[t, places[t][0][i] + places[t][1][j]].astype(F32)
            out[i * unit:(i + 1) * unit, j * unit:(j + 1) * unit] = total

        @pl.when(r < 2)
        def _():
            span = slice(i * unit, (i + 1) * unit)
            panel[pa, span] = out[span, :].astype(BF16)
            for j in range(i * unit // chunk, (i + 1) * unit // chunk):
                send_panel(j)

    row_hops = lax.div(r, 2)
    at_pa = HOP_ROW * row_hops
    at_pb = at_pa + HOP_ROW
    line_pa = at_pa + HOP_CORE + HOP_COL * chip_hops
    line_pb = at_pb + HOP_COL * chip_hops
    at_carried = jnp.where(on_line, line_pb, line_pa)
    at_other = jnp.where(diag, at_pa, jnp.where(on_line, line_pa, line_pb) + HOP_CORE)
    ready = jnp.maximum(jnp.maximum(at_carried, at_other), at_pb)
    steps = 2 * CHUNKS + ready

    def step(h, carry):
        def due(first):
            j = lax.div(h - first + 2, 2) - 1
            return j, (h >= first) & (j < CHUNKS) & (lax.rem(h - first + 2 * CHUNKS, 2) == 0)

        j_pa, do_pa = due(at_pa)

        @pl.when(do_pa & (r >= 2))
        def _():
            panel_got(pa, j_pa)
            send_panel(j_pa)

        @pl.when(do_pa & diag)
        def _():
            divide(pa, j_pa)
            left_copy(pa, j_pa, sibling, core_send).start()

        j_pb, do_pb = due(at_pb)

        @pl.when(do_pb & diag)
        def _():
            panel_got(pb, j_pb)
            divide(pb, j_pb)
            along(j_pb)
            left_copy(pb, j_pb, sibling, core_send).start()

        j_c, do_c = due(at_carried)

        @pl.when(do_c & jnp.logical_not(diag))
        def _():
            left_copy(pc, j_c, sibling, core_send).wait_recv()
            along(j_c)

            @pl.when(jnp.logical_not(at_source))
            def _():
                left_copy(pc, j_c, sibling, core_send).start()

        j_m, do_m = due(ready)

        @pl.when(do_m & jnp.logical_not(diag))
        def _():
            panel_got(pb, j_m)
            left_copy(po, j_m, sibling, core_send).wait_recv()

        @pl.when(do_m & (lax.rem(j_m, MERGE) == MERGE - 1))
        def _():
          first = pl.multiple_of((j_m - (MERGE - 1)) * chunk, MERGE * chunk)
          at = pl.ds(first, MERGE * chunk)
          factor = jnp.concatenate([left[p, at] for p in range(2)], axis=0)
          right = jnp.concatenate([panel[p, at] for p in range(2)], axis=0)
          out[...] = out[...] - contract0(factor, right)
        return carry

    lax.fori_loop(0, steps, step, 0)

    pltpu.make_async_copy(send.at[pl.ds(0, rows - 1)], recv.at[pl.ds(0, rows - 1)], t_send).wait()

    def drained(ref, sem):
        pltpu.make_async_copy(ref, ref, sem).wait()

    drained(panel.at[0], ax_send)

    @pl.when(r + 2 < rows)
    def _():
        drained(panel.at[0], ay_send)

    @pl.when(has_up)
    def _():
        drained(left.at[0], up_send)

    @pl.when(has_dn)
    def _():
        drained(left.at[0], dn_send)

    @pl.when(diag)
    def _():
        drained(left, core_send)

    @pl.when(jnp.logical_not(at_source))
    def _():
        drained(left.at[0], core_send)


def body(rows, cols, inverses, coupling, orders, owners, offsets, dense_slab, pivots):
    subs, order = inverses.shape[1], inverses.shape[2]
    width, tile = coupling.shape[3], dense_slab.shape[0]
    unit = (tile - width) // 2
    nb = width // unit
    packed = nb * nb // 2 * unit + nb // 2 * PAD
    panel_width = pivots.shape[0]
    assert nb % 2 == 0 and panel_width == 2 * tile and rows % 2 == 0 and cols % 2 == 0
    dma = pltpu.SemaphoreType.DMA
    hbm = pl.BlockSpec(memory_space=pl.ANY)
    smem = pl.BlockSpec(memory_space=pltpu.SMEM)
    vmem = pl.BlockSpec(memory_space=pltpu.VMEM)
    return pl.pallas_call(
        functools.partial(kernel, (rows, cols, subs, order, width, tile)),
        out_shape=pltpu.VMEM((tile, tile), F32),
        in_specs=[hbm, hbm, smem, smem, smem, hbm, vmem],
        out_specs=vmem,
        scratch_shapes=[
            pltpu.VMEM((subs, order, order), BF16),
            pltpu.VMEM((subs, order, width), BF16),
            pltpu.VMEM((tile, tile), F32),
            pltpu.VMEM((rows, packed, unit), BF16),
            pltpu.VMEM((rows, packed, unit), BF16),
            pltpu.VMEM((rows, (nb + 1) * (nb + 1), unit, unit), BF16),
            pltpu.VMEM((2, tile, tile), BF16),
            pltpu.VMEM((2, tile, tile), BF16),
            pltpu.VMEM((panel_width, 128), F32),
            dma((subs,)), dma((subs,)), dma(()),
            dma(()), dma((rows,)),
            dma(()), dma(()), dma((2, CHUNKS)),
            dma(()), dma(()), dma(()), dma((2, CHUNKS)),
        ],
        compiler_params=pltpu.CompilerParams(collective_id=0, has_side_effects=True),
    )(inverses, coupling, orders, jnp.transpose(owners, (0, 2, 1)),
      jnp.transpose(offsets, (0, 2, 1)), dense_slab, pivots.reshape(-1, 128))


def solution(mesh):
    placed = (
        P("row", "col", None, None),
        P("row", "col", None, None),
        P("row", "col"),
        P(None, "col", None),
        P(None, "col", None),
        P("row", "col"),
        P(),
    )
    return jax.shard_map(
        functools.partial(body, mesh.shape["row"], mesh.shape["col"]),
        mesh=mesh, in_specs=placed, out_specs=P("row", "col"), check_vma=False)
```

time: 38.3 us -> 35.3 us (0.922)
  Pallas kernels: 37.1 us -> 34.2 us
    pallas_call x1, Pallas kernels: 37.1 us -> 34.2 us  [body(): pl.pallas_call(functools.partial(kernel, (rows, cols, subs, order, width,...]
where the time goes in v1:
time: 35.3 us; the launch traced here: 35.2 us
  Pallas kernels  34.2 us (97%)
  local copies, waits for them, and re-layouts  0.97 us (3%)
    pallas_call x1, Pallas kernels, body(): pl.pallas_call(functools.partial(kernel, (rows, cols, subs, order, width,...  34.2 us
    unnamed x1, local copies, waits for them, and re-layouts  0.97 us

profile of v1, /device:TPU:29, one launch (start us, length us, event | category | flops | bytes accessed | tf_op | source)
XLA Modules:
  0.0 35.2 jit_solution(14675504145306577160)
XLA Ops:
  0.0 34.2 %shard_map.73 = f32[512,512]{1,0:T(8,128)S(1)} custom-call(bf16[1,4,1024,1024]{3,2,1,0:T(8,128)(2,1)} %inv_hbm.1, bf16[1,4,1024,256]{3,2,1,0:T(8,128)(2,1)} %cpl_hbm.1, s32[1,4]{1,0:T(1,128)} %orders.1, s32[4,1,4]{2,1,0:T(1,128)} %bitcast.7, s32[4,2,4]{2,1,0:T(2,128)} %bitcast.5, f32[512,512]{1,0:T(8,128)} %slab_hbm.1, f32[8,128]{1,0:T(8,128)} %bitcast.6), custom_call_target="tpu_custom_call" | custom-call | tf_op jit(solution)/shard_map/pallas_call | solution.py:366
  34.2 1.0 %copy.10 = f32[512,512]{1,0:T(8,128)} copy(f32[512,512]{1,0:T(8,128)S(1)} %shard_map.73) | data formatting | bytes 2097152

commit v2 on v1

--- a/solution.py
+++ b/solution.py
@@ -13,9 +13,9 @@
 MERGE = 2
 AB = 256
 PAD = 16
-HOP_ROW = 8
-HOP_COL = 8
-HOP_CORE = 5
+HOP_ROW = 4
+HOP_COL = 4
+HOP_CORE = 2
 
 
 def contract0(a, b):
@@ -24,10 +24,11 @@
 
 def kernel(
     dims,
-    inv_hbm, cpl_hbm, orders, owners, offsets, slab_hbm, pivots,
+    inv_hbm, cpl_hbm, orders_hbm, owners_hbm, offsets_hbm, slab_hbm, pivots_hbm,
     out,
+    orders, owners, offsets, pivots,
     a_buf, m_buf, slab, send, recv, placed, panel, left, piv,
-    a_sem, m_sem, s_sem, t_send, t_recv, ax_send, ay_send, g_recv,
+    a_sem, m_sem, s_sem, i_sem, t_send, t_recv, ax_send, ay_send, g_recv,
     up_send, dn_send, core_send, l_recv,
 ):
     rows, cols, subs, order, width, tile = dims
@@ -56,25 +57,25 @@
     pc = jnp.where(on_line, pb, pa)
     po = 1 - pc
 
-    def load_a(s, i):
+    def load_a(i):
+        rows_i, cols_i = pl.ds(i * AB, AB), pl.ds(i * AB, order - i * AB)
         return pltpu.make_async_copy(
-            inv_hbm.at[0, s, pl.ds(i * AB, AB), pl.ds(i * AB, order - i * AB)],
-            a_buf.at[s, pl.ds(i * AB, AB), pl.ds(i * AB, order - i * AB)],
-            a_sem.at[s])
-
-    def wait_a(s):
+            inv_hbm.at[0, :, rows_i, cols_i], a_buf.at[:, rows_i, cols_i], a_sem)
+
+    def wait_a():
         total = sum(AB * (order - i * AB) for i in range(ablocks)) // order
         pltpu.make_async_copy(
-            inv_hbm.at[0, s, pl.ds(0, total)], a_buf.at[s, pl.ds(0, total)], a_sem.at[s]).wait()
-
-    def load_m(s):
-        return pltpu.make_async_copy(cpl_hbm.at[0, s], m_buf.at[s], m_sem.at[s])
-
+            inv_hbm.at[0, :, pl.ds(0, total)], a_buf.at[:, pl.ds(0, total)], a_sem).wait()
+
+    load_m = pltpu.make_async_copy(cpl_hbm.at[0], m_buf, m_sem)
     load_slab = pltpu.make_async_copy(slab_hbm, slab, s_sem)
-    for s in range(subs):
-        load_m(s).start()
-        for i in range(ablocks):
-            load_a(s, i).start()
+    small = [pltpu.make_async_copy(src, dst, i_sem.at[k]) for k, (src, dst) in enumerate(
+        ((orders_hbm, orders), (owners_hbm, owners), (offsets_hbm, offsets), (pivots_hbm, pivots)))]
+    load_m.start()
+    for i in range(ablocks):
+        load_a(i).start()
+    for copy in small:
+        copy.start()
 
     barrier = pltpu.get_barrier_semaphore()
     for t in range(rows):
@@ -135,9 +136,10 @@
                                     (PAD, unit)) for a in range(1, nb, 2)]
         return jnp.concatenate(stored, axis=0).astype(BF16)
 
-    for s in range(subs):
-        load_m(s).wait()
-        wait_a(s)
+    load_m.wait()
+    wait_a()
+    for copy in small:
+        copy.wait()
     load_slab.start()
 
     neighbours = rows + jnp.where(q + 1 < chips, 1, 0) + jnp.where(q > 0, 1, 0)
@@ -185,11 +187,10 @@
             device_id=(mate, c), device_id_type=MESH).wait_recv()
 
     def send_panel(j):
+        @pl.when(r + 2 < rows)
+        def _():
+            panel_copy(j, r + 2, ay_send).start()
         panel_copy(j, mate, ax_send).start()
-
-        @pl.when(r + 2 < rows)
-        def _():
-            panel_copy(j, r + 2, ay_send).start()
 
     def left_copy(p, j, target, sem):
         return pltpu.make_async_remote_copy(
@@ -266,12 +267,12 @@
     at_carried = jnp.where(on_line, line_pb, line_pa)
     at_other = jnp.where(diag, at_pa, jnp.where(on_line, line_pa, line_pb) + HOP_CORE)
     ready = jnp.maximum(jnp.maximum(at_carried, at_other), at_pb)
-    steps = 2 * CHUNKS + ready
+    steps = CHUNKS + ready
 
     def step(h, carry):
         def due(first):
-            j = lax.div(h - first + 2, 2) - 1
-            return j, (h >= first) & (j < CHUNKS) & (lax.rem(h - first + 2 * CHUNKS, 2) == 0)
+            j = h - first
+            return j, (j >= 0) & (j < CHUNKS)
 
         j_pa, do_pa = due(at_pa)
 
@@ -361,14 +362,17 @@
     assert nb % 2 == 0 and panel_width == 2 * tile and rows % 2 == 0 and cols % 2 == 0
     dma = pltpu.SemaphoreType.DMA
     hbm = pl.BlockSpec(memory_space=pl.ANY)
-    smem = pl.BlockSpec(memory_space=pltpu.SMEM)
     vmem = pl.BlockSpec(memory_space=pltpu.VMEM)
     return pl.pallas_call(
         functools.partial(kernel, (rows, cols, subs, order, width, tile)),
         out_shape=pltpu.VMEM((tile, tile), F32),
-        in_specs=[hbm, hbm, smem, smem, smem, hbm, vmem],
+        in_specs=[hbm] * 7,
         out_specs=vmem,
         scratch_shapes=[
+            pltpu.SMEM(orders.shape, jnp.int32),
+            pltpu.SMEM((owners.shape[0], owners.shape[2], owners.shape[1]), jnp.int32),
+            pltpu.SMEM((offsets.shape[0], offsets.shape[2], offsets.shape[1]), jnp.int32),
+            pltpu.VMEM((panel_width // 128, 128), F32),
             pltpu.VMEM((subs, order, order), BF16),
             pltpu.VMEM((subs, order, width), BF16),
             pltpu.VMEM((tile, tile), F32),
@@ -378,7 +382,7 @@
             pltpu.VMEM((2, tile, tile), BF16),
             pltpu.VMEM((2, tile, tile), BF16),
             pltpu.VMEM((panel_width, 128), F32),
-            dma((subs,)), dma((subs,)), dma(()),
+            dma(()), dma(()), dma(()), dma((4,)),
             dma(()), dma((rows,)),
             dma(()), dma(()), dma((2, CHUNKS)),
             dma(()), dma(()), dma(()), dma((2, CHUNKS)),

time: 35.3 us -> 34.2 us (0.969)
  Pallas kernels: 34.2 us -> 33.1 us
    pallas_call x1, Pallas kernels: 34.2 us -> 33.1 us  [body(): pl.pallas_call(functools.partial(kernel, (rows, cols, subs, order, width,...]
where the time goes in v2:
time: 34.2 us; the launch traced here: 34.1 us
  Pallas kernels  33.1 us (97%)
  local copies, waits for them, and re-layouts  0.97 us (3%)
    pallas_call x1, Pallas kernels, body(): pl.pallas_call(functools.partial(kernel, (rows, cols, subs, order, width,...  33.1 us
    unnamed x1, local copies, waits for them, and re-layouts  0.97 us

profile of v2, /device:TPU:29, one launch (start us, length us, event | category | flops | bytes accessed | tf_op | source)
XLA Modules:
  0.0 34.1 jit_solution(12271952271957157182)
XLA Ops:
  0.0 33.1 %shard_map.73 = f32[512,512]{1,0:T(8,128)S(1)} custom-call(bf16[1,4,1024,1024]{3,2,1,0:T(8,128)(2,1)} %inv_hbm.1, bf16[1,4,1024,256]{3,2,1,0:T(8,128)(2,1)} %cpl_hbm.1, s32[1,4]{1,0:T(1,128)} %orders_hbm.1, s32[4,1,4]{2,1,0:T(1,128)} %bitcast.7, s32[4,2,4]{2,1,0:T(2,128)} %bitcast.5, f32[512,512]{1,0:T(8,128)} %slab_hbm.1, f32[8,128]{1,0:T(8,128)} %bitcast.6), custom_call_target="tpu_custom_call" | custom-call | tf_op jit(solution)/shard_map/pallas_call | solution.py:366
  33.1 1.0 %copy.10 = f32[512,512]{1,0:T(8,128)} copy(f32[512,512]{1,0:T(8,128)S(1)} %shard_map.73) | data formatting | bytes 2097152

commit v3 on v2

--- a/solution.py
+++ b/solution.py
@@ -13,9 +13,10 @@
 MERGE = 2
 AB = 256
 PAD = 16
-HOP_ROW = 4
+HOP_ROW = 2
+HOP_MATE = 4
 HOP_COL = 4
-HOP_CORE = 2
+HOP_CORE = 3
 
 
 def contract0(a, b):
@@ -261,7 +262,7 @@
 
     row_hops = lax.div(r, 2)
     at_pa = HOP_ROW * row_hops
-    at_pb = at_pa + HOP_ROW
+    at_pb = at_pa + HOP_MATE
     line_pa = at_pa + HOP_CORE + HOP_COL * chip_hops
     line_pb = at_pb + HOP_COL * chip_hops
     at_carried = jnp.where(on_line, line_pb, line_pa)

time: 34.2 us -> 34.2 us (level)
  no operation moved by 1% of the time
where the time goes in v3:
time: 34.2 us; the launch traced here: 34.1 us
  Pallas kernels  33.1 us (97%)
  local copies, waits for them, and re-layouts  0.97 us (3%)
    pallas_call x1, Pallas kernels, body(): pl.pallas_call(functools.partial(kernel, (rows, cols, subs, order, width,...  33.1 us
    unnamed x1, local copies, waits for them, and re-layouts  0.97 us

profile of v3, /device:TPU:29, one launch (start us, length us, event | category | flops | bytes accessed | tf_op | source)
XLA Modules:
  0.0 34.1 jit_solution(13703620963081014593)
XLA Ops:
  0.0 33.1 %shard_map.73 = f32[512,512]{1,0:T(8,128)S(1)} custom-call(bf16[1,4,1024,1024]{3,2,1,0:T(8,128)(2,1)} %inv_hbm.1, bf16[1,4,1024,256]{3,2,1,0:T(8,128)(2,1)} %cpl_hbm.1, s32[1,4]{1,0:T(1,128)} %orders_hbm.1, s32[4,1,4]{2,1,0:T(1,128)} %bitcast.7, s32[4,2,4]{2,1,0:T(2,128)} %bitcast.5, f32[512,512]{1,0:T(8,128)} %slab_hbm.1, f32[8,128]{1,0:T(8,128)} %bitcast.6), custom_call_target="tpu_custom_call" | custom-call | tf_op jit(solution)/shard_map/pallas_call | solution.py:367
  33.1 1.0 %copy.10 = f32[512,512]{1,0:T(8,128)} copy(f32[512,512]{1,0:T(8,128)S(1)} %shard_map.73) | data formatting | bytes 2097152
